TPU v7x, 32 devices: a whole 2x2x4 slice. The times are simulated.
32 devices in a mesh: box: 8 (over z, y), face: 4 (over x, core).
Axes of the slice: x: 2, y: 2, z: 4, core: 2. Of those that a mesh axis runs over, the one named last changes fastest.
Arguments:
- blocks: bfloat16 [32, 24, 24, 128, 128], P('box', 'face'), may hold values from -1 to 2
- pattern: int32 [32, 24, 24], P('box', 'face'), may hold values from 0 to 1, as said below
- shared: int32 [32, 4], P('box'), may hold values from 0 to 23, as said below
- sketch: bfloat16 [3072, 256], replicated, may hold values from -6 to 6
Outputs:
- merged: bfloat16 [32, 3072, 256], P('box', 'face')
Inputs may be any that keep to these rules, and one draw needn't show every extreme that they name: `pattern`: 1 where a block is stored; every diagonal block is stored. `shared`: 4 distinct block indices in increasing order.
All inputs are finite; a program needn't handle non-finite values.
Results may differ from a plain program's by a relative error of at most 0.0085.
Values may be sent and summed in bfloat16 or wider, within the bound.
No kernel may reach another device: no remote copies, remote signals or barrier semaphores. Data moves between devices by JAX's collectives and lax.ppermute only.
A program may use at most 128 MiB of HBM per device.

v0:
```python
import jax
import jax.numpy as jnp
from jax import lax
from jax.sharding import PartitionSpec as P

ITERS = 4


def partner(value, axis, stride):
    mask = 2**stride
    pairs = [(source, source ^ mask) for source in range(lax.axis_size(axis))]
    return lax.ppermute(value, axis, pairs)


def local(blocks, pattern, shared, sketch):
    box_count, row_blocks, all_blocks, blk_size, _ = blocks.shape
    col_count = sketch.shape[1]
    row_start = lax.axis_index("face") * row_blocks
    block_ids = lax.iota(jnp.int32, all_blocks)
    rows_here = row_start + lax.iota(jnp.int32, row_blocks)
    chosen = shared[:, :, None] == block_ids[None, None, :]
    exterior = 1 - jnp.any(chosen, axis=1).astype(jnp.int32)
    keep_ext = (pattern * exterior[:, None, :]).astype(blocks.dtype)
    kept_ext = blocks * keep_ext[:, :, :, None, None]
    sketch_blocks = sketch.reshape(all_blocks, blk_size, col_count)
    sketched = jnp.einsum(
        "brjpq,jqc->brpc", kept_ext, sketch_blocks, preferred_element_type=jnp.float32
    ).astype(jnp.bfloat16)
    column_pick = chosen.astype(jnp.bfloat16)
    side_cols = jnp.einsum(
        "brjpq,bkj->brkpq", blocks, column_pick, preferred_element_type=jnp.float32
    )
    side_mask = jnp.einsum(
        "brj,bkj->brk",
        pattern.astype(jnp.float32),
        chosen.astype(jnp.float32),
        precision=lax.Precision.HIGHEST,
    )
    side_cols = (side_cols * side_mask[:, :, :, None, None]).astype(jnp.bfloat16)
    row_pick_b16 = (shared[:, :, None] == rows_here[None, None, :]).astype(jnp.bfloat16)
    slot_y = jnp.einsum(
        "bkr,brpc->bkpc", row_pick_b16, sketched, preferred_element_type=jnp.float32
    )
    slot_side = jnp.einsum(
        "bkr,brlpq->bklpq", row_pick_b16, side_cols, preferred_element_type=jnp.float32
    )
    here_y, here_side = (
        lax.psum(slot_y.astype(jnp.bfloat16), "face").astype(jnp.float32),
        lax.psum(slot_side.astype(jnp.bfloat16), "face").astype(jnp.float32),
    )
    there_y, there_side = partner(
        (here_y.astype(jnp.bfloat16), here_side.astype(jnp.bfloat16)), "box", 0
    )
    right_side = here_y + there_y.astype(jnp.float32)
    system = here_side + there_side.astype(jnp.float32)
    diag_sum = jnp.diagonal(jnp.diagonal(system, axis1=1, axis2=2), axis1=1, axis2=2)
    part_cols = col_count // lax.axis_size("face")
    col_start = lax.axis_index("face") * part_cols
    part_rhs = lax.dynamic_slice_in_dim(right_side, col_start, part_cols, 3)
    potential = part_rhs / diag_sum[..., None]
    for sweep_index in range(ITERS - 1):
        applied = jnp.einsum("bklpq,blqc->bkpc", system, potential, precision=lax.Precision.HIGHEST)
        potential = potential + (part_rhs - applied) / diag_sum[..., None]
    potential = lax.all_gather(potential.astype(jnp.bfloat16), "face", axis=3, tiled=True).astype(
        potential.dtype
    )
    correction = jnp.einsum(
        "brkpq,bkqc->brpc",
        side_cols,
        potential.astype(jnp.bfloat16),
        preferred_element_type=jnp.float32,
    )
    merged = (sketched.astype(jnp.float32) - correction).astype(jnp.bfloat16)
    return merged.reshape(box_count, row_blocks * blk_size, col_count)


def solution(mesh):
    return jax.shard_map(
        local,
        mesh=mesh,
        in_specs=(P("box", "face", None, None, None), P("box", "face", None), P("box", None), P()),
        out_specs=P("box", "face", None),
        check_vma=False,
    )
```

profile of v0, /device:TPU:0, one launch (start us, length us, event | category | flops | bytes accessed | tf_op | source)
XLA Modules:
  0.0 247.8 jit_solution(17600785656989528693)
XLA Ops:
  6.5 0.9 fusion.40
  7.4 0.8 fusion.49
  8.2 0.9 convolution_bitcast_fusion
  9.1 0.1 copy.62
  9.2 25.3 %fusion = f32[4,4,6,128,128]{4,1,3,2,0:T(4,128)} fusion(bf16[4,6,24,128,128]{4,3,2,1,0:T(8,128)(2,1)} %param.4, s32[4,4]{1,0:T(4,128)} %param.6), kind=kOutput, calls=%fused_computation.2 | convolution fusion | flops 75497856 | bytes 25165888 | tf_op jit(solution)/shard_map/brjpq,bkj->brkpq/dot_general | solution.py:30
  34.5 3.8 %fusion.5 = bf16[4,6,4,128,128]{4,3,2,1,0:T(8,128)(2,1)S(1)} fusion(f32[4,4,6,128,128]{4,1,3,2,0:T(4,128)} %fusion, f32[4,6,4]{2,1,0:T(8,128)S(1)} %copy.62), kind=kLoop, calls=%fused_computation.8 | loop fusion | flops 3145728 | bytes 9437568 | tf_op jit(solution)/shard_map/convert_element_type | solution.py:39
  38.3 2.3 fusion.6
  40.6 1.9 copy.98
  42.5 2.1 copy-done.2
  44.6 5.5 %bitcast_convert_fusion = bf16[4,6,128,256]{3,2,1,0:T(8,128)(2,1)S(1)} fusion(bf16[24,128,256,1,1]{2,1,0,4,3:T(8,128)(2,1)S(1)} %bitcast.90, bf16[4,6,24,128,128]{4,3,2,1,0:T(8,128)(2,1)S(1)} %copy-done.2, bf16[4,6,24]{2,1,0:T(8,128)(2,1)S(1)} %copy.58), kind=kOutput, calls=%fused_computation.19 | convolution fusion | flops 4842061824 | bytes 22021248 | tf_op jit(solution)/shard_map/brjpq,jqc->brpc/dot_general | solution.py:26
  50.0 1.2 fusion.13
  51.2 1.5 copy.64
  52.7 0.0 all-reduce.3.cloned.1.call-update
  52.7 0.0 all-gather.2.cloned.1.call-start
  52.8 71.3 %all-reduce.3.cloned.1.call-done = (bf16[4,4,4,128,128]{4,3,2,1,0:T(8,128)(2,1)}, bf16[4,4,128,256]{2,3,1,0:T(8,128)(2,1)}) async-done(((bf16[4,4,4,128,128]{4,3,2,1,0:T(8,128)(2,1)}, bf16[4,4,128,256]{2,3,1,0:T(8,128)(2,1)}), (bf16[4,4,4,128,128]{4,3,2,1,0:T(8,128)(2,1)}, bf16[4,4,128,256]{2,3,1,0:T(8,128)(2,1)})) %all-reduce.3.cloned.1.call-update) | async-done | bytes 3145744 | tf_op jit(solution)/shard_map/psum | solution.py:49
  124.1 1.5 collective-permute-start.1
  125.5 0.6 collective-permute-start
  126.1 46.8 %collective-permute-done.1 = bf16[4,4,4,128,128]{4,3,2,1,0:T(8,128)(2,1)} collective-permute-done((bf16[4,4,4,128,128]{4,3,2,1,0:T(8,128)(2,1)}, bf16[4,4,4,128,128]{4,3,2,1,0:T(8,128)(2,1)}, u32[]{:S(2)}, u32[]{:S(2)}) %collective-permute-start.1) | collective-permute-done | bytes 2097184 | tf_op jit(solution)/shard_map/ppermute | solution.py:12
  172.9 5.0 %fusion.11 = f32[4,128,128,4,4]{2,1,4,3,0:T(8,128)} fusion(bf16[4,4,4,128,128]{4,3,2,1,0:T(8,128)(2,1)} %collective-permute-done.1, bf16[4,4,4,128,128]{4,3,2,1,0:T(8,128)(2,1)} %get-tuple-element.5), kind=kLoop, calls=%fused_computation.16 | loop fusion | flops 3145728 | bytes 8388608 | tf_op jit(solution)/shard_map/jit(diagonal)/transpose | solution.py:56
  177.9 2.8 %gather_fusion = f32[4,4,128,128]{3,2,1,0:T(8,128)S(1)} fusion(f32[4,128,128,4,4]{2,1,4,3,0:T(8,128)} %fusion.11, s32[4]{0:T(128)S(1)} %or_bitcast_fusion.1), kind=kCustom, calls=%fused_computation | custom fusion | bytes 2097184 | tf_op jit(solution)/shard_map/jit(diagonal)/gather | solution.py:56
  180.7 16.5 %copy.67 = f32[4,4,128,128]{1,0,3,2:T(4,128)} copy(f32[4,4,128,128]{3,2,0,1:T(8,128)S(1)} %bitcast.91) | data formatting | bytes 2097152 | tf_op jit(solution)/shard_map/jit(diagonal)/transpose | solution.py:56
  197.2 1.9 gather_fusion.1
  199.1 0.1 copy.68
  199.2 0.0 collective-permute-done
  199.2 7.1 %fusion.24 = f32[4,4,128,64]{2,3,1,0:T(8,128)S(1)} fusion(bf16[4,4,4,128,128]{4,3,2,1,0:T(8,128)(2,1)} %collective-permute-done.1, bf16[4,4,4,128,128]{4,3,2,1,0:T(8,128)(2,1)} %get-tuple-element.5, f32[4,4,128]{2,1,0:T(4,128)S(1)} %copy.68, bf16[4,4,128,256]{2,3,1,0:T(8,128)(2,1)} %collective-permute-done, s32[]{:T(128)S(6)} %select_n.11, ...), kind=kOutput, calls=%fused_computation.29 | convolution fusion | flops 809893888 | bytes 5784576 | tf_op jit(solution)/shard_map/bklpq,blqc->bkpc/dot_general | solution.py:62
  206.4 0.0 copy-done.4
  206.4 6.1 %fusion.26 = f32[4,4,128,64]{2,3,1,0:T(8,128)S(1)} fusion(f32[4,4,128,64]{2,3,1,0:T(8,128)S(1)} %fusion.24, bf16[4,4,4,128,128]{4,3,2,1,0:T(8,128)(2,1)} %collective-permute-done.1, bf16[4,4,4,128,128]{4,3,2,1,0:T(8,128)(2,1)S(1)} %copy-done.4, f32[4,4,128]{2,1,0:T(4,128)S(1)} %copy.68, bf16[4,4,128,256]{2,3,1,0:T(8,128)(2,1)} %collective-permute-done, ...), kind=kOutput, calls=%fused_computation.31 | convolution fusion | flops 809238528 | bytes 6299652 | tf_op jit(solution)/shard_map/bklpq,blqc->bkpc/dot_general | solution.py:62
  212.5 6.1 %fusion.29 = bf16[4,4,128,64]{2,3,1,0:T(8,128)(2,1)S(1)} fusion(f32[4,4,128,64]{2,3,1,0:T(8,128)S(1)} %fusion.26, bf16[4,4,4,128,128]{4,3,2,1,0:T(8,128)(2,1)} %collective-permute-done.1, bf16[4,4,4,128,128]{4,3,2,1,0:T(8,128)(2,1)S(1)} %copy-done.4, f32[4,4,128]{2,1,0:T(4,128)S(1)} %copy.68, bf16[4,4,128,256]{2,3,1,0:T(8,128)(2,1)} %collective-permute-done, ...), kind=kOutput, calls=%fused_computation.34 | convolution fusion | flops 809369600 | bytes 6037508 | tf_op jit(solution)/shard_map/bklpq,blqc->bkpc/dot_general | solution.py:62
  218.6 0.9 copy.69
  219.5 0.0 all-gather.2.cloned.1.call-update
  219.5 16.9 %all-gather.2.cloned.1.call-done = bf16[4,4,128,256]{2,1,0,3:T(4,128)(2,1)} async-done(((bf16[4,4,128,64]{2,1,0,3:T(4,128)(2,1)}), bf16[4,4,128,256]{2,1,0,3:T(4,128)(2,1)}) %all-gather.2.cloned.1.call-update) | async-done | bytes 1048592 | tf_op jit(solution)/shard_map/all_gather | solution.py:64
  236.5 4.5 %fusion.12 = bf16[4,6,128,256]{3,2,1,0:T(8,128)(2,1)} fusion(bf16[4,6,128,256]{3,2,1,0:T(8,128)(2,1)S(1)} %bitcast_convert_fusion, bf16[4,6,4,128,128]{4,3,2,1,0:T(8,128)(2,1)} %copy-done.3, bf16[4,4,128,256,1]{2,1,0,3,4:T(4,128)(2,1)} %bitcast.93), kind=kOutput, calls=%fused_computation.18 | convolution fusion | flops 807665664 | bytes 7340032 | tf_op jit(solution)/shard_map/brkpq,bkqc->brpc/dot_general | solution.py:67
  (18 shorter events, 0.1 us)
Async XLA Ops:
  6.5 36.0 %copy-start = (bf16[3072,256]{1,0:T(8,128)(2,1)S(1)}, bf16[3072,256]{1,0:T(8,128)(2,1)}, u32[]{:S(2)}) copy-start(bf16[3072,256]{1,0:T(8,128)(2,1)} %param.7) | copy-start | bytes 4718596
  6.5 117.5 %all-reduce.3.cloned.1.call-start = ((), (), s32[]{:S(2)}) async-start(), calls=%async_computation.1 | async-start | bytes 6291456 | tf_op jit(solution)/shard_map/psum | solution.py:49
  9.2 29.1 %copy-start.5 = (s32[4,4]{1,0:T(4,128)S(1)}, s32[4,4]{1,0:T(4,128)}, u32[]{:S(2)}) copy-start(s32[4,4]{1,0:T(4,128)} %param.6) | copy-start | bytes 196
  34.5 10.1 %copy-start.2 = (bf16[4,6,24,128,128]{4,3,2,1,0:T(8,128)(2,1)S(1)}, bf16[4,6,24,128,128]{4,3,2,1,0:T(8,128)(2,1)}, u32[]{:S(2)}) copy-start(bf16[4,6,24,128,128]{4,3,2,1,0:T(8,128)(2,1)} %param.4) | copy-start | bytes 56623108
  38.3 2.3 copy-start.3
  52.7 183.8 %all-gather.2.cloned.1.call-start = ((), (), s32[]{:S(2)}) async-start(), calls=%async_computation | async-start | bytes 1310720 | tf_op jit(solution)/shard_map/all_gather | solution.py:64
  124.1 48.8 %collective-permute-start.1 = (bf16[4,4,4,128,128]{4,3,2,1,0:T(8,128)(2,1)}, bf16[4,4,4,128,128]{4,3,2,1,0:T(8,128)(2,1)}, u32[]{:S(2)}, u32[]{:S(2)}) collective-permute-start(bf16[4,4,4,128,128]{4,3,2,1,0:T(8,128)(2,1)} %get-tuple-element.5), channel_id=1, source_target_pairs={{0,4},{4,0},{8,12},{12,8},{16,20},{20,16},{24,28},{28,24},{1,5},{5... | collective-permute-start | bytes 6291464 | tf_op jit(solution)/shard_map/ppermute | solution.py:12
  125.5 73.7 %collective-permute-start = (bf16[4,4,128,256]{2,3,1,0:T(8,128)(2,1)}, bf16[4,4,128,256]{2,3,1,0:T(8,128)(2,1)}, u32[]{:S(2)}, u32[]{:S(2)}) collective-permute-start(bf16[4,4,128,256]{2,3,1,0:T(8,128)(2,1)} %get-tuple-element.6), channel_id=1, source_target_pairs={{0,4},{4,0},{8,12},{12,8},{16,20},{20,16},{24,28},{28,24},{1,5},{5... | collective-permute-start | bytes 3145736 | tf_op jit(solution)/shard_map/ppermute | solution.py:12
  199.2 7.2 %copy-start.4 = (bf16[4,4,4,128,128]{4,3,2,1,0:T(8,128)(2,1)S(1)}, bf16[4,4,4,128,128]{4,3,2,1,0:T(8,128)(2,1)}, u32[]{:S(2)}) copy-start(bf16[4,4,4,128,128]{4,3,2,1,0:T(8,128)(2,1)} %get-tuple-element.5) | copy-start | bytes 6291460
  199.2 7.2 %copy-start.6 = (bf16[4,4,128,256]{2,3,1,0:T(8,128)(2,1)S(1)}, bf16[4,4,128,256]{2,3,1,0:T(8,128)(2,1)}, u32[]{:S(2)}) copy-start(bf16[4,4,128,256]{2,3,1,0:T(8,128)(2,1)} %get-tuple-element.6) | copy-start | bytes 3145732
  236.5 4.5 %copy-start.1 = (bf16[3072,256]{1,0:T(8,128)(2,1)S(1)}, bf16[3072,256]{1,0:T(8,128)(2,1)}, u32[]{:S(2)}) copy-start(bf16[3072,256]{1,0:T(8,128)(2,1)} %param.7) | copy-start | bytes 4718596
Sparse Core Ops, SparseCore 0:
  52.8 71.1 all-reduce.2
  219.7 16.7 all-gather.1
where the time goes:
time: 248 us
  waiting for transfers between devices  135 us (54%)
  matrix products  58.9 us (24%)
  local copies, waits for them, and re-layouts  27.7 us (11%)
  between operations  13.5 us (5%)
  other arithmetic  10.5 us (4%)
    psum x1, waiting for transfers between devices, local(): lax.psum(slot_side.astype(jnp.bfloat16), 'face').astype(jnp.float32)  71.3 us
    ppermute x2, waiting for transfers between devices, partner(): return lax.ppermute(value, axis, pairs)  46.8 us
    dot_general x1, matrix products, local(): jnp.einsum('brjpq,bkj->brkpq', blocks, column_pick, preferred_element_typ...  25.3 us
    dot_general x3, matrix products, local(): jnp.einsum('bklpq,blqc->bkpc', system, potential, precision=lax.Precision...  19.4 us
    all_gather x1, waiting for transfers between devices, local(): lax.all_gather(potential.astype(jnp.bfloat16), 'face', axis=3, tiled=True)  16.9 us
    transpose x1, local copies, waits for them, and re-layouts, local(): jnp.diagonal(jnp.diagonal(system, axis1=1, axis2=2), axis1=1, axis2=2)  16.5 us
    dot_general x1, matrix products, local(): jnp.einsum('brjpq,jqc->brpc', kept_ext, sketch_blocks, preferred_element_...  5.47 us
    transpose x1, other arithmetic, local(): jnp.diagonal(system, axis1=1, axis2=2)  4.99 us
  transfers between devices with their start and end apart: 4, of which 3 were waited for; matrix products, arithmetic and copies ran while one was open for 11% of the time, Pallas kernels for 0%

commit v1 on v0

--- a/solution.py
+++ b/solution.py
@@ -46,7 +46,7 @@
     )
     here_y, here_side = (
         lax.psum(slot_y.astype(jnp.bfloat16), "face").astype(jnp.float32),
-        lax.psum(slot_side.astype(jnp.bfloat16), "face").astype(jnp.float32),
+        jnp.sum(lax.all_gather(slot_side.astype(jnp.bfloat16), "face"), axis=0).astype(jnp.float32),
     )
     there_y, there_side = partner(
         (here_y.astype(jnp.bfloat16), here_side.astype(jnp.bfloat16)), "box", 0

time: 248 us -> 233 us (0.940)
  waiting for transfers between devices: 135 us -> 113 us
  other arithmetic: 10.5 us -> 17.6 us
    all_gather x0 -> x1, waiting for transfers between devices: none -> 60.9 us  [local(): lax.all_gather(slot_side.astype(jnp.bfloat16), 'face')]
    ppermute x2, waiting for transfers between devices: 46.8 us -> 0.02 us  [partner(): return lax.ppermute(value, axis, pairs)]
    psum x1, waiting for transfers between devices: 71.3 us -> 35.7 us  [local(): lax.psum(slot_y.astype(jnp.bfloat16), 'face').astype(jnp.float32)]
    reduce_sum x0 -> x1, other arithmetic: none -> 7.26 us  [local(): jnp.sum(lax.all_gather(slot_side.astype(jnp.bfloat16), 'face'), axis=0)]
    dot_general x1, matrix products: 5.47 us -> 9.1 us  [local(): jnp.einsum('brjpq,jqc->brpc', kept_ext, sketch_blocks, preferred_element_...]
  transfers between devices with their start and end apart: 4 -> 5, of which waited for: 3 -> 3; matrix products, arithmetic and copies ran while one was open for 11% -> 16% of each run, Pallas kernels for 0% -> 0%
where the time goes in v1:
time: 233 us
  waiting for transfers between devices  113 us (48%)
  matrix products  60.2 us (26%)
  local copies, waits for them, and re-layouts  25.7 us (11%)
  other arithmetic  17.6 us (8%)
  between operations  13.2 us (6%)
  starting transfers between devices  3.21 us (1%)
    all_gather x1, waiting for transfers between devices, local(): lax.all_gather(slot_side.astype(jnp.bfloat16), 'face')  60.9 us
    psum x1, waiting for transfers between devices, local(): lax.psum(slot_y.astype(jnp.bfloat16), 'face').astype(jnp.float32)  35.7 us
    dot_general x1, matrix products, local(): jnp.einsum('brjpq,bkj->brkpq', blocks, column_pick, preferred_element_typ...  23 us
    dot_general x3, matrix products, local(): jnp.einsum('bklpq,blqc->bkpc', system, potential, precision=lax.Precision...  19.4 us
    transpose x1, local copies, waits for them, and re-layouts, local(): jnp.diagonal(jnp.diagonal(system, axis1=1, axis2=2), axis1=1, axis2=2)  16.5 us
    all_gather x1, waiting for transfers between devices, local(): lax.all_gather(potential.astype(jnp.bfloat16), 'face', axis=3, tiled=True)  16.1 us
    dot_general x1, matrix products, local(): jnp.einsum('brjpq,jqc->brpc', kept_ext, sketch_blocks, preferred_element_...  9.1 us
    reduce_sum x1, other arithmetic, local(): jnp.sum(lax.all_gather(slot_side.astype(jnp.bfloat16), 'face'), axis=0)  7.26 us
  transfers between devices with their start and end apart: 5, of which 3 were waited for; matrix products, arithmetic and copies ran while one was open for 16% of the time, Pallas kernels for 0%

profile of v1, /device:TPU:0, one launch (start us, length us, event | category | flops | bytes accessed | tf_op | source)
XLA Modules:
  0.0 232.8 jit_solution(10451698992959360161)
XLA Ops:
  6.5 0.9 fusion.43
  7.4 0.8 fusion.52
  8.2 0.9 convolution_bitcast_fusion
  9.1 0.1 copy.71
  9.2 23.0 %fusion = f32[4,4,6,128,128]{4,1,3,2,0:T(4,128)} fusion(bf16[4,6,24,128,128]{4,3,2,1,0:T(8,128)(2,1)} %param.4, s32[4,4]{1,0:T(4,128)} %param.6), kind=kOutput, calls=%fused_computation.2 | convolution fusion | flops 75497856 | bytes 25165888 | tf_op jit(solution)/shard_map/brjpq,bkj->brkpq/dot_general | solution.py:30
  32.2 3.6 %fusion.5 = bf16[4,6,4,128,128]{4,3,2,1,0:T(8,128)(2,1)S(1)} fusion(f32[4,4,6,128,128]{4,1,3,2,0:T(4,128)} %fusion, f32[4,6,4]{2,1,0:T(8,128)S(1)} %copy.71), kind=kLoop, calls=%fused_computation.8 | loop fusion | flops 3145728 | bytes 9437568 | tf_op jit(solution)/shard_map/convert_element_type | solution.py:39
  35.8 2.3 fusion.15
  38.1 1.9 copy.75
  40.0 0.0 all-gather.6.cloned.1.call-update
  40.1 0.2 all-reduce.2.cloned.1.call-start
  40.3 60.9 %all-gather.6.cloned.1.call-done = bf16[16,4,4,128,128]{4,3,2,1,0:T(8,128)(2,1)} async-done(((bf16[4,4,4,128,128]{4,3,2,1,0:T(8,128)(2,1)}), bf16[16,4,4,128,128]{4,3,2,1,0:T(8,128)(2,1)}) %all-gather.6.cloned.1.call-update) | async-done | bytes 8388624 | tf_op jit(solution)/shard_map/all_gather | solution.py:49
  101.2 7.3 %reduce_sum.12 = bf16[4,4,4,128,128]{4,3,2,1,0:T(8,128)(2,1)} reduce(bf16[4,4,4,4,128,128]{5,4,3,2,1,0:T(8,128)(2,1)} %bitcast.93, bf16[]{:T(256)} %constant.28.clone.1), dimensions={0}, to_apply=%region_2.0 | reduce | flops 3145728 | bytes 10485762 | tf_op jit(solution)/shard_map/reduce_sum | solution.py:49
  108.5 1.5 collective-permute-start.1
  109.9 9.1 %bitcast_convert_fusion = bf16[4,6,128,256]{3,2,1,0:T(8,128)(2,1)S(1)} fusion(bf16[24,128,256,1,1]{2,1,0,4,3:T(8,128)(2,1)S(1)} %bitcast.91, bf16[4,6,24,128,128]{4,3,2,1,0:T(8,128)(2,1)} %param.4, bf16[4,6,24]{2,1,0:T(8,128)(2,1)S(1)} %copy.67), kind=kOutput, calls=%fused_computation.18 | convolution fusion | flops 4842061824 | bytes 22021248 | tf_op jit(solution)/shard_map/brjpq,jqc->brpc/dot_general | solution.py:26
  119.0 1.2 fusion.13
  120.2 1.5 copy.73
  121.7 0.0 all-gather.4.cloned.1.call-start
  121.8 35.7 %all-reduce.2.cloned.1.call-done = bf16[4,4,128,256]{2,3,1,0:T(8,128)(2,1)} async-done(((bf16[4,4,128,256]{2,3,1,0:T(8,128)(2,1)}), bf16[4,4,128,256]{2,3,1,0:T(8,128)(2,1)}) %all-reduce.2.cloned.1.call-update) | async-done | bytes 1048592 | tf_op jit(solution)/shard_map/psum | solution.py:48
  157.5 1.5 collective-permute-start
  159.0 5.0 %fusion.11 = f32[4,128,128,4,4]{2,1,4,3,0:T(8,128)} fusion(bf16[4,4,4,128,128]{4,3,2,1,0:T(8,128)(2,1)} %collective-permute-done.1, bf16[4,4,4,128,128]{4,3,2,1,0:T(8,128)(2,1)} %reduce_sum.12), kind=kLoop, calls=%fused_computation.15 | loop fusion | flops 3145728 | bytes 8388608 | tf_op jit(solution)/shard_map/jit(diagonal)/transpose | solution.py:56
  164.0 2.8 %gather_fusion = f32[4,4,128,128]{3,2,1,0:T(8,128)S(1)} fusion(f32[4,128,128,4,4]{2,1,4,3,0:T(8,128)} %fusion.11, s32[4]{0:T(128)S(1)} %or_bitcast_fusion.1), kind=kCustom, calls=%fused_computation | custom fusion | bytes 2097184 | tf_op jit(solution)/shard_map/jit(diagonal)/gather | solution.py:56
  166.8 16.5 %copy.79 = f32[4,4,128,128]{1,0,3,2:T(4,128)} copy(f32[4,4,128,128]{3,2,0,1:T(8,128)S(1)} %bitcast.92) | data formatting | bytes 2097152 | tf_op jit(solution)/shard_map/jit(diagonal)/transpose | solution.py:56
  183.3 1.9 gather_fusion.1
  185.2 0.1 copy.80
  185.3 0.0 collective-permute-done
  185.4 7.1 %fusion.27 = f32[4,4,128,64]{2,3,1,0:T(8,128)S(1)} fusion(bf16[4,4,4,128,128]{4,3,2,1,0:T(8,128)(2,1)} %collective-permute-done.1, bf16[4,4,4,128,128]{4,3,2,1,0:T(8,128)(2,1)} %reduce_sum.12, f32[4,4,128]{2,1,0:T(4,128)S(1)} %copy.80, bf16[4,4,128,256]{2,3,1,0:T(8,128)(2,1)} %collective-permute-done, s32[]{:T(128)S(6)} %select_n.11, ...), kind=kOutput, calls=%fused_computation.29 | convolution fusion | flops 809893888 | bytes 5784576 | tf_op jit(solution)/shard_map/bklpq,blqc->bkpc/dot_general | solution.py:62
  192.5 6.1 %fusion.29 = f32[4,4,128,64]{2,3,1,0:T(8,128)S(1)} fusion(f32[4,4,128,64]{2,3,1,0:T(8,128)S(1)} %fusion.27, bf16[4,4,4,128,128]{4,3,2,1,0:T(8,128)(2,1)} %collective-permute-done.1, bf16[4,4,4,128,128]{4,3,2,1,0:T(8,128)(2,1)S(1)} %copy-done.3, f32[4,4,128]{2,1,0:T(4,128)S(1)} %copy.80, bf16[4,4,128,256]{2,3,1,0:T(8,128)(2,1)} %collective-permute-done, ...), kind=kOutput, calls=%fused_computation.31 | convolution fusion | flops 809238528 | bytes 6299652 | tf_op jit(solution)/shard_map/bklpq,blqc->bkpc/dot_general | solution.py:62
  198.6 6.1 %fusion.32 = bf16[4,4,128,64]{2,3,1,0:T(8,128)(2,1)S(1)} fusion(f32[4,4,128,64]{2,3,1,0:T(8,128)S(1)} %fusion.29, bf16[4,4,4,128,128]{4,3,2,1,0:T(8,128)(2,1)} %collective-permute-done.1, bf16[4,4,4,128,128]{4,3,2,1,0:T(8,128)(2,1)S(1)} %copy-done.3, f32[4,4,128]{2,1,0:T(4,128)S(1)} %copy.80, bf16[4,4,128,256]{2,3,1,0:T(8,128)(2,1)} %collective-permute-done, ...), kind=kOutput, calls=%fused_computation.34 | convolution fusion | flops 809369600 | bytes 6037508 | tf_op jit(solution)/shard_map/bklpq,blqc->bkpc/dot_general | solution.py:62
  204.8 0.9 copy.81
  205.7 0.0 all-gather.4.cloned.1.call-update
  205.7 16.1 %all-gather.4.cloned.1.call-done = bf16[4,4,128,256]{2,1,0,3:T(4,128)(2,1)} async-done(((bf16[4,4,128,64]{2,1,0,3:T(4,128)(2,1)}), bf16[4,4,128,256]{2,1,0,3:T(4,128)(2,1)}) %all-gather.4.cloned.1.call-update) | async-done | bytes 1048592 | tf_op jit(solution)/shard_map/all_gather | solution.py:64
  221.8 4.5 %fusion.12 = bf16[4,6,128,256]{3,2,1,0:T(8,128)(2,1)} fusion(bf16[4,6,128,256]{3,2,1,0:T(8,128)(2,1)S(1)} %bitcast_convert_fusion, bf16[4,6,4,128,128]{4,3,2,1,0:T(8,128)(2,1)} %copy-done.2, bf16[4,4,128,256,1]{2,1,0,3,4:T(4,128)(2,1)} %bitcast.95), kind=kOutput, calls=%fused_computation.17 | convolution fusion | flops 807665664 | bytes 7340032 | tf_op jit(solution)/shard_map/brkpq,bkqc->brpc/dot_general | solution.py:67
  (20 shorter events, 0.1 us)
Async XLA Ops:
  6.5 103.4 %copy-start = (bf16[3072,256]{1,0:T(8,128)(2,1)S(1)}, bf16[3072,256]{1,0:T(8,128)(2,1)}, u32[]{:S(2)}) copy-start(bf16[3072,256]{1,0:T(8,128)(2,1)} %param.7) | copy-start | bytes 4718596
  6.5 94.7 %all-gather.6.cloned.1.call-start = ((), (), s32[]{:S(2)}) async-start(), calls=%async_computation.2 | async-start | bytes 10485760 | tf_op jit(solution)/shard_map/all_gather | solution.py:49
  32.2 3.7 %copy-start.4 = (s32[4,4]{1,0:T(4,128)S(1)}, s32[4,4]{1,0:T(4,128)}, u32[]{:S(2)}) copy-start(s32[4,4]{1,0:T(4,128)} %param.6) | copy-start | bytes 196
  35.8 2.3 copy-start.2
  40.1 117.5 %all-reduce.2.cloned.1.call-start = ((), (), s32[]{:S(2)}) async-start(), calls=%async_computation | async-start | bytes 2097152 | tf_op jit(solution)/shard_map/psum | solution.py:48
  108.5 50.6 %collective-permute-start.1 = (bf16[4,4,4,128,128]{4,3,2,1,0:T(8,128)(2,1)}, bf16[4,4,4,128,128]{4,3,2,1,0:T(8,128)(2,1)}, u32[]{:S(2)}, u32[]{:S(2)}) collective-permute-start(bf16[4,4,4,128,128]{4,3,2,1,0:T(8,128)(2,1)} %reduce_sum.12), channel_id=1, source_target_pairs={{0,4},{4,0},{8,12},{12,8},{16,20},{20,16},{24,28},{28,24},{1,5},{5... | collective-permute-start | bytes 6291464 | tf_op jit(solution)/shard_map/ppermute | solution.py:12
  121.7 100.1 %all-gather.4.cloned.1.call-start = ((), (), s32[]{:S(2)}) async-start(), calls=%async_computation.1 | async-start | bytes 1310720 | tf_op jit(solution)/shard_map/all_gather | solution.py:64
  157.5 27.8 %collective-permute-start = (bf16[4,4,128,256]{2,3,1,0:T(8,128)(2,1)}, bf16[4,4,128,256]{2,3,1,0:T(8,128)(2,1)}, u32[]{:S(2)}, u32[]{:S(2)}) collective-permute-start(bf16[4,4,128,256]{2,3,1,0:T(8,128)(2,1)} %all-reduce.2.cloned.1.call-done), channel_id=1, source_target_pairs={{0,4},{4,0},{8,12},{12,8},{16,20},{20,16},{24,28},{28,24},{1,5},{5... | collective-permute-start | bytes 3145736 | tf_op jit(solution)/shard_map/ppermute | solution.py:12
  185.3 7.2 %copy-start.3 = (bf16[4,4,4,128,128]{4,3,2,1,0:T(8,128)(2,1)S(1)}, bf16[4,4,4,128,128]{4,3,2,1,0:T(8,128)(2,1)}, u32[]{:S(2)}) copy-start(bf16[4,4,4,128,128]{4,3,2,1,0:T(8,128)(2,1)} %reduce_sum.12) | copy-start | bytes 6291460
  185.3 7.2 %copy-start.5 = (bf16[4,4,128,256]{2,3,1,0:T(8,128)(2,1)S(1)}, bf16[4,4,128,256]{2,3,1,0:T(8,128)(2,1)}, u32[]{:S(2)}) copy-start(bf16[4,4,128,256]{2,3,1,0:T(8,128)(2,1)} %all-reduce.2.cloned.1.call-done) | copy-start | bytes 3145732
  221.8 4.5 %copy-start.1 = (bf16[3072,256]{1,0:T(8,128)(2,1)S(1)}, bf16[3072,256]{1,0:T(8,128)(2,1)}, u32[]{:S(2)}) copy-start(bf16[3072,256]{1,0:T(8,128)(2,1)} %param.7) | copy-start | bytes 4718596
Sparse Core Ops, SparseCore 0:
  40.2 60.9 all-gather.5
  121.8 35.6 all-reduce.1
  205.8 15.9 all-gather.3
